TPU v7x, 256 devices: a whole 4x4x8 slice. The times are simulated.
256 devices in a mesh: section: 2 (over y_hi), seq: 32 (over x, z), chan: 4 (over y_lo, core).
Axes of the slice: x: 4, y: 4 (y_hi: 2, y_lo: 2; y = y_hi * 2 + y_lo), z: 8, core: 2. Of those that a mesh axis runs over, the one named last changes fastest.
Arguments:
- bases: int32 [2, 2097152], P('section', 'seq'), may hold values from 0 to 3
- stem_embedding_weight: bfloat16 [512, 1536], P(None, 'chan'), may hold values from -1.64443437 to 1.64443437
- gains: float32 [3, 1536], replicated, may hold values from 0.1 to 1.9
- conv_weight: bfloat16 [3, 3, 1536, 1536], P(None, None, None, 'chan'), may hold values from -0.09375 to 0.09375
- dec_weight: bfloat16 [1536, 384], P('chan'), may hold values from -0.3125 to 0.3125
- upstream: bfloat16 [2, 16384, 1536], P('section', 'seq', 'chan'), may hold values from -0.032958984 to 0.032958984
Outputs:
- decoded: bfloat16 [2, 16384, 1536], P('section', 'seq', 'chan')
- weight_grad: float32 [1536, 384], P('chan')
All inputs are finite; a program needn't handle non-finite values.
Results may differ from a plain program's by a relative error of at most 0.0076.
Values may be sent and summed in bfloat16 or wider, within the bound.
No kernel may reach another device: no remote copies, remote signals or barrier semaphores. Data moves between devices by JAX's collectives and lax.ppermute only.
A program may use at most 128 MiB of HBM per device.

v0:
```python
import jax
import jax.numpy as jnp
from jax import lax
from jax.sharding import PartitionSpec as P

PATCH = 128
FIRST_DILATION0 = 2
EPSILON = 1e-06


def with_halo(shard, sides, width):
    for axis, dim in sides:
        size, length = (lax.axis_size(axis), shard.shape[dim])
        up = [(i, (i + 1) % size) for i in range(size - 1)]
        down = [(j, i) for i, j in up]
        last = lax.slice_in_dim(shard, length - width, length, axis=dim)
        initial = lax.slice_in_dim(shard, 0, width, axis=dim)
        before = lax.ppermute(last, axis, up)
        after = lax.ppermute(initial, axis, down)
        shard = jnp.concatenate([before, shard, after], axis=dim)
    return shard


def activate(rows, gain_row):
    widened = rows.astype(jnp.float32)
    inverse_rms = lax.rsqrt(jnp.mean(widened * widened, axis=-1, keepdims=True) + EPSILON)
    return jax.nn.gelu(widened * inverse_rms * gain_row).astype(jnp.bfloat16)


def apply_convolution(padded, kernel_taps, dilation_step, row_count):
    update = jnp.dot(padded[0:row_count], kernel_taps[0], preferred_element_type=jnp.float32)
    for offset in range(1, kernel_taps.shape[0]):
        start = offset * dilation_step
        update = update + jnp.dot(
            padded[start : start + row_count],
            kernel_taps[offset],
            preferred_element_type=jnp.float32,
        )
    return update


def body(bases, stem_embedding_weight, gains, conv_weight, dec_weight, upstream):
    row_count = upstream.shape[1]
    letters = bases.reshape(row_count, PATCH)
    onehot = letters[:, :, None] == jnp.arange(4, dtype=jnp.int32)[None, None, :]
    onehot = onehot.astype(jnp.bfloat16).reshape(row_count, PATCH * 4)
    stream = jnp.dot(onehot, stem_embedding_weight, preferred_element_type=jnp.float32).astype(
        jnp.bfloat16
    )
    for tower_layer_index in range(conv_weight.shape[0]):
        dilation_step = FIRST_DILATION0 * 2**tower_layer_index
        full_rows = lax.all_gather(stream, "chan", axis=1, tiled=True)
        padded = with_halo(
            activate(full_rows, gains[tower_layer_index]), (("seq", 0),), dilation_step
        )
        update = apply_convolution(padded, conv_weight[tower_layer_index], dilation_step, row_count)
        stream = (stream.astype(jnp.float32) + update).astype(jnp.bfloat16)
    decoded = jnp.dot(stream, dec_weight, preferred_element_type=jnp.float32).astype(jnp.bfloat16)
    upstream_rows = upstream[0]
    contract_row_pairs = (((0,), (0,)), ((), ()))
    partial_grad = lax.dot_general(
        stream, upstream_rows, contract_row_pairs, preferred_element_type=jnp.float32
    )
    weight_grad = lax.psum(partial_grad, ("section", "seq"))
    return (decoded[None], weight_grad)


def solution(mesh):
    placed = (
        P("section", "seq"),
        P(None, "chan"),
        P(),
        P(None, None, None, "chan"),
        P("chan", None),
        P("section", "seq", "chan"),
    )
    return jax.shard_map(
        body,
        mesh=mesh,
        in_specs=placed,
        out_specs=(P("section", "seq", "chan"), P("chan", None)),
        check_vma=False,
    )
```

profile of v0, /device:TPU:24, one launch (start us, length us, event | category | flops | bytes accessed | tf_op | source)
XLA Modules:
  0.0 813.8 jit_solution(4729358638135030658)
XLA Ops:
  10.5 29.4 %all-gather.4.cloned.1.call-done = bf16[512,1536]{1,0:T(8,128)(2,1)} async-done(((bf16[512,384]{1,0:T(8,128)(2,1)}), bf16[512,1536]{1,0:T(8,128)(2,1)}) %all-gather.4.cloned.1.call-update) | async-done | bytes 1572880 | tf_op jit(solution)/shard_map/all_gather | solution.py:52
  39.8 1.8 fusion
  41.6 2.8 fusion.4
  44.5 3.5 collective-permute-start
  49.2 2.2 fusion.60
  51.5 2.0 collective-permute-done.1
  53.4 2.3 fusion.38
  55.7 3.1 fusion.49
  58.8 28.8 %all-gather.6.cloned.1.call-done = bf16[512,1536]{1,0:T(8,128)(2,1)} async-done(((bf16[512,384]{1,0:T(8,128)(2,1)}), bf16[512,1536]{1,0:T(8,128)(2,1)}) %all-gather.6.cloned.1.call-update) | async-done | bytes 1572880 | tf_op jit(solution)/shard_map/all_gather | solution.py:52
  87.6 1.8 fusion.9
  89.4 2.8 fusion.13
  93.5 2.2 fusion.56
  95.8 4.7 collective-permute-start.2
  100.5 2.3 fusion.34
  102.8 3.0 add_convert_fusion.1
  105.9 29.4 %all-gather.8.cloned.1.call-done = bf16[512,1536]{1,0:T(8,128)(2,1)} async-done(((bf16[512,384]{1,0:T(8,128)(2,1)}), bf16[512,1536]{1,0:T(8,128)(2,1)}) %all-gather.8.cloned.1.call-update) | async-done | bytes 1572880 | tf_op jit(solution)/shard_map/all_gather | solution.py:52
  135.3 1.8 fusion.18
  137.1 2.8 fusion.22
  141.4 2.2 fusion.52
  143.7 4.7 collective-permute-start.4
  148.4 2.2 fusion.30
  150.7 2.3 add_convert_fusion
  155.4 649.9 %all-reduce.2.cloned.1.call-done = f32[384,384]{1,0:T(8,128)} async-done(((f32[384,384]{1,0:T(8,128)}), f32[384,384]{1,0:T(8,128)}) %all-reduce.2.cloned.1.call-update) | async-done | bytes 589840 | tf_op jit(solution)/shard_map/psum | solution.py:64
  805.3 1.9 copy.10
  (45 shorter events, 9.9 us)
Async XLA Ops:
  7.2 1.8 copy-start
  7.2 3.2 copy-start.6
  7.2 32.7 %all-gather.4.cloned.1.call-start = ((), (), s32[]{:S(2)}) async-start(), calls=%async_computation | async-start | bytes 1966080 | tf_op jit(solution)/shard_map/all_gather | solution.py:52
  10.4 77.3 %all-gather.6.cloned.1.call-start = ((), (), s32[]{:S(2)}) async-start(), calls=%async_computation.1 | async-start | bytes 1966080 | tf_op jit(solution)/shard_map/all_gather | solution.py:52
  44.5 11.2 %collective-permute-start = (bf16[2,1536]{1,0:T(2,128)(2,1)S(1)}, bf16[2,1536]{1,0:T(2,128)(2,1)S(1)}, u32[]{:S(2)}, u32[]{:S(2)}) collective-permute-start(bf16[2,1536]{1,0:T(2,128)(2,1)S(1)} %get-tuple-element.9), channel_id=1, source_target_pairs={{0,4},{4,8},{8,12},{12,16},{16,20},{20,24},{24,28},{28,32},{32,36}... | collective-permute-start | bytes 18440 | tf_op jit(solution)/shard_map/ppermute | solution.py:18
  47.9 5.5 collective-permute-start.1
  51.5 4.2 copy-start.1
  58.8 76.5 %all-gather.8.cloned.1.call-start = ((), (), s32[]{:S(2)}) async-start(), calls=%async_computation.2 | async-start | bytes 1966080 | tf_op jit(solution)/shard_map/all_gather | solution.py:52
  92.2 8.3 %collective-permute-start.3 = (bf16[4,1536]{1,0:T(4,128)(2,1)S(1)}, bf16[4,1536]{1,0:T(4,128)(2,1)S(1)}, u32[]{:S(2)}, u32[]{:S(2)}) collective-permute-start(bf16[4,1536]{1,0:T(4,128)(2,1)S(1)} %get-tuple-element.8), channel_id=1, source_target_pairs={{4,0},{8,4},{12,8},{16,12},{20,16},{24,20},{28,24},{32,28},{36,32}... | collective-permute-start | bytes 36872 | tf_op jit(solution)/shard_map/ppermute | solution.py:19
  95.8 7.0 copy-start.3
  95.8 7.0 collective-permute-start.2
  105.9 699.5 %all-reduce.2.cloned.1.call-start = ((), (), s32[]{:S(2)}) async-start(), calls=%async_computation.3 | async-start | bytes 1179648 | tf_op jit(solution)/shard_map/psum | solution.py:64
  139.9 8.4 %collective-permute-start.5 = (bf16[8,1536]{1,0:T(8,128)(2,1)S(1)}, bf16[8,1536]{1,0:T(8,128)(2,1)S(1)}, u32[]{:S(2)}, u32[]{:S(2)}) collective-permute-start(bf16[8,1536]{1,0:T(8,128)(2,1)S(1)} %get-tuple-element.6), channel_id=1, source_target_pairs={{4,0},{8,4},{12,8},{16,12},{20,16},{24,20},{28,24},{32,28},{36,32}... | collective-permute-start | bytes 73736 | tf_op jit(solution)/shard_map/ppermute | solution.py:19
  143.7 7.0 copy-start.2
  143.7 7.0 collective-permute-start.4
  150.6 2.4 copy-start.4
  150.6 3.6 copy-start.5
Sparse Core Ops, SparseCore 0:
  10.5 29.3 all-gather.3
  58.9 28.6 all-gather.5
  106.0 29.3 all-gather.7
  154.4 650.8 all-reduce.1
where the time goes:
time: 815 us; the launch traced here: 814 us
  waiting for transfers between devices  740 us (91%)
  matrix products  25.6 us (3%)
  starting transfers between devices  17 us (2%)
  between operations  14.1 us (2%)
  other arithmetic  13.7 us (2%)
    psum x1, waiting for transfers between devices, body(): weight_grad = lax.psum(partial_grad, ('section', 'seq'))  650 us
    all_gather x3, waiting for transfers between devices, body(): full_rows = lax.all_gather(stream, 'chan', axis=1, tiled=True)  87.6 us
  transfers between devices with their start and end apart: 10, of which 5 were waited for; matrix products, arithmetic and copies ran while one was open for 2% of the time, Pallas kernels for 0%

commit v1 on v0

--- a/solution.py
+++ b/solution.py
@@ -61,7 +61,7 @@
     partial_grad = lax.dot_general(
         stream, upstream_rows, contract_row_pairs, preferred_element_type=jnp.float32
     )
-    weight_grad = lax.psum(partial_grad, ("section", "seq"))
+    weight_grad = lax.psum(lax.psum(partial_grad, "seq"), "section")
     return (decoded[None], weight_grad)
 
 

time: 815 us -> 358 us (0.44)
  waiting for transfers between devices: 740 us -> 281 us
    psum x1 -> x2, waiting for transfers between devices: 650 us -> 191 us  [body(): weight_grad = lax.psum(lax.psum(partial_grad, 'seq'), 'section')]
  transfers between devices with their start and end apart: 10 -> 11, of which waited for: 5 -> 6; matrix products, arithmetic and copies ran while one was open for 2% -> 4% of each run, Pallas kernels for 0% -> 0%
where the time goes in v1:
time: 358 us; the launch traced here: 355 us
  waiting for transfers between devices  281 us (78%)
  matrix products  25.6 us (7%)
  starting transfers between devices  17.1 us (5%)
  between operations  14.1 us (4%)
  other arithmetic  13.7 us (4%)
  local copies, waits for them, and re-layouts  3.78 us (1%)
    psum x2, waiting for transfers between devices, body(): weight_grad = lax.psum(lax.psum(partial_grad, 'seq'), 'section')  191 us
    all_gather x3, waiting for transfers between devices, body(): full_rows = lax.all_gather(stream, 'chan', axis=1, tiled=True)  87.6 us
    dot_general x6, matrix products, apply_convolution(): jnp.dot(padded[start:start + row_count], kernel_taps[offset], preferred_e...  13.5 us
    ppermute x3, starting transfers between devices, with_halo(): before = lax.ppermute(last, axis, up)  12.8 us
    dot_general x3, matrix products, apply_convolution(): jnp.dot(padded[0:row_count], kernel_taps[0], preferred_element_type=jnp.f...  8.45 us
    convert_element_type x3, other arithmetic, activate(): return jax.nn.gelu(widened * inverse_rms * gain_row).astype(jnp.bfloat16)  8.35 us
  transfers between devices with their start and end apart: 11, of which 6 were waited for; matrix products, arithmetic and copies ran while one was open for 4% of the time, Pallas kernels for 0%

profile of v1, /device:TPU:24, one launch (start us, length us, event | category | flops | bytes accessed | tf_op | source)
XLA Modules:
  0.0 354.9 jit_solution(6602686329960665526)
XLA Ops:
  10.5 29.4 %all-gather.4.cloned.1.call-done = bf16[512,1536]{1,0:T(8,128)(2,1)} async-done(((bf16[512,384]{1,0:T(8,128)(2,1)}), bf16[512,1536]{1,0:T(8,128)(2,1)}) %all-gather.4.cloned.1.call-update) | async-done | bytes 1572880 | tf_op jit(solution)/shard_map/all_gather | solution.py:52
  39.8 1.8 fusion
  41.6 2.8 fusion.4
  44.5 3.5 collective-permute-start
  49.2 2.2 fusion.60
  51.5 2.0 collective-permute-done.1
  53.4 2.3 fusion.38
  55.7 3.1 fusion.49
  58.8 28.8 %all-gather.6.cloned.1.call-done = bf16[512,1536]{1,0:T(8,128)(2,1)} async-done(((bf16[512,384]{1,0:T(8,128)(2,1)}), bf16[512,1536]{1,0:T(8,128)(2,1)}) %all-gather.6.cloned.1.call-update) | async-done | bytes 1572880 | tf_op jit(solution)/shard_map/all_gather | solution.py:52
  89.4 2.8 fusion.13
  93.5 2.2 fusion.56
  95.8 4.7 %collective-permute-start.2 = (bf16[4,1536]{1,0:T(4,128)(2,1)S(1)}, bf16[4,1536]{1,0:T(4,128)(2,1)S(1)}, u32[]{:S(2)}, u32[]{:S(2)}) collective-permute-start(bf16[4,1536]{1,0:T(4,128)(2,1)S(1)} %get-tuple-element.7), channel_id=1, source_target_pairs={{0,4},{4,8},{8,12},{12,16},{16,20},{20,24},{24,28},{28,32},{32,36}... | collective-permute-start | bytes 36872 | tf_op jit(solution)/shard_map/ppermute | solution.py:18
  100.5 2.3 fusion.34
  102.8 3.0 add_convert_fusion.1
  105.9 29.4 %all-gather.8.cloned.1.call-done = bf16[512,1536]{1,0:T(8,128)(2,1)} async-done(((bf16[512,384]{1,0:T(8,128)(2,1)}), bf16[512,1536]{1,0:T(8,128)(2,1)}) %all-gather.8.cloned.1.call-update) | async-done | bytes 1572880 | tf_op jit(solution)/shard_map/all_gather | solution.py:52
  135.3 1.8 fusion.18
  137.1 2.8 fusion.22
  141.4 2.2 fusion.52
  143.7 4.7 %collective-permute-start.4 = (bf16[8,1536]{1,0:T(8,128)(2,1)S(1)}, bf16[8,1536]{1,0:T(8,128)(2,1)S(1)}, u32[]{:S(2)}, u32[]{:S(2)}) collective-permute-start(bf16[8,1536]{1,0:T(8,128)(2,1)S(1)} %get-tuple-element.5), channel_id=1, source_target_pairs={{0,4},{4,8},{8,12},{12,16},{16,20},{20,24},{24,28},{28,32},{32,36}... | collective-permute-start | bytes 73736 | tf_op jit(solution)/shard_map/ppermute | solution.py:18
  148.4 2.2 fusion.30
  150.7 2.3 add_convert_fusion
  154.3 150.3 %all-reduce.3.cloned.1.call-done = f32[384,384]{1,0:T(8,128)} async-done(((f32[384,384]{1,0:T(8,128)}), f32[384,384]{1,0:T(8,128)}) %all-reduce.3.cloned.1.call-update) | async-done | bytes 589840 | tf_op jit(solution)/shard_map/psum | solution.py:64
  305.8 40.6 %all-reduce.5.cloned.1.call-done = f32[384,384]{1,0:T(8,128)} async-done(((f32[384,384]{1,0:T(8,128)}), f32[384,384]{1,0:T(8,128)}) %all-reduce.5.cloned.1.call-update) | async-done | bytes 589840 | tf_op jit(solution)/shard_map/psum | solution.py:64
  346.4 1.9 copy.11
  (48 shorter events, 11.7 us)
Async XLA Ops:
  7.2 1.8 copy-start
  7.2 3.2 copy-start.6
  7.2 32.7 %all-gather.4.cloned.1.call-start = ((), (), s32[]{:S(2)}) async-start(), calls=%async_computation | async-start | bytes 1966080 | tf_op jit(solution)/shard_map/all_gather | solution.py:52
  10.4 77.3 %all-gather.6.cloned.1.call-start = ((), (), s32[]{:S(2)}) async-start(), calls=%async_computation.1 | async-start | bytes 1966080 | tf_op jit(solution)/shard_map/all_gather | solution.py:52
  44.5 11.2 %collective-permute-start = (bf16[2,1536]{1,0:T(2,128)(2,1)S(1)}, bf16[2,1536]{1,0:T(2,128)(2,1)S(1)}, u32[]{:S(2)}, u32[]{:S(2)}) collective-permute-start(bf16[2,1536]{1,0:T(2,128)(2,1)S(1)} %get-tuple-element.9), channel_id=1, source_target_pairs={{0,4},{4,8},{8,12},{12,16},{16,20},{20,24},{24,28},{28,32},{32,36}... | collective-permute-start | bytes 18440 | tf_op jit(solution)/shard_map/ppermute | solution.py:18
  47.9 5.5 %collective-permute-start.1 = (bf16[2,1536]{1,0:T(2,128)(2,1)S(1)}, bf16[2,1536]{1,0:T(2,128)(2,1)S(1)}, u32[]{:S(2)}, u32[]{:S(2)}) collective-permute-start(bf16[2,1536]{1,0:T(2,128)(2,1)S(1)} %get-tuple-element.10), channel_id=1, source_target_pairs={{4,0},{8,4},{12,8},{16,12},{20,16},{24,20},{28,24},{32,28},{36,32}... | collective-permute-start | bytes 18440 | tf_op jit(solution)/shard_map/ppermute | solution.py:19
  51.5 4.2 %copy-start.1 = (bf16[512,384]{1,0:T(8,128)(2,1)S(1)}, bf16[512,384]{1,0:T(8,128)(2,1)}, u32[]{:S(2)}) copy-start(bf16[512,384]{1,0:T(8,128)(2,1)} %convolution_convert_fusion.1) | copy-start | bytes 1179652
  58.8 76.5 %all-gather.8.cloned.1.call-start = ((), (), s32[]{:S(2)}) async-start(), calls=%async_computation.2 | async-start | bytes 1966080 | tf_op jit(solution)/shard_map/all_gather | solution.py:52
  92.2 8.3 %collective-permute-start.3 = (bf16[4,1536]{1,0:T(4,128)(2,1)S(1)}, bf16[4,1536]{1,0:T(4,128)(2,1)S(1)}, u32[]{:S(2)}, u32[]{:S(2)}) collective-permute-start(bf16[4,1536]{1,0:T(4,128)(2,1)S(1)} %get-tuple-element.8), channel_id=1, source_target_pairs={{4,0},{8,4},{12,8},{16,12},{20,16},{24,20},{28,24},{32,28},{36,32}... | collective-permute-start | bytes 36872 | tf_op jit(solution)/shard_map/ppermute | solution.py:19
  95.8 7.0 %copy-start.3 = (bf16[512,384]{1,0:T(8,128)(2,1)S(1)}, bf16[512,384]{1,0:T(8,128)(2,1)}, u32[]{:S(2)}) copy-start(bf16[512,384]{1,0:T(8,128)(2,1)} %fusion.49) | copy-start | bytes 1179652
  95.8 7.0 %collective-permute-start.2 = (bf16[4,1536]{1,0:T(4,128)(2,1)S(1)}, bf16[4,1536]{1,0:T(4,128)(2,1)S(1)}, u32[]{:S(2)}, u32[]{:S(2)}) collective-permute-start(bf16[4,1536]{1,0:T(4,128)(2,1)S(1)} %get-tuple-element.7), channel_id=1, source_target_pairs={{0,4},{4,8},{8,12},{12,16},{16,20},{20,24},{24,28},{28,32},{32,36}... | collective-permute-start | bytes 36872 | tf_op jit(solution)/shard_map/ppermute | solution.py:18
  105.9 198.8 %all-reduce.3.cloned.1.call-start = ((), (), s32[]{:S(2)}) async-start(), calls=%async_computation.3 | async-start | bytes 1179648 | tf_op jit(solution)/shard_map/psum | solution.py:64
  139.9 8.4 %collective-permute-start.5 = (bf16[8,1536]{1,0:T(8,128)(2,1)S(1)}, bf16[8,1536]{1,0:T(8,128)(2,1)S(1)}, u32[]{:S(2)}, u32[]{:S(2)}) collective-permute-start(bf16[8,1536]{1,0:T(8,128)(2,1)S(1)} %get-tuple-element.6), channel_id=1, source_target_pairs={{4,0},{8,4},{12,8},{16,12},{20,16},{24,20},{28,24},{32,28},{36,32}... | collective-permute-start | bytes 73736 | tf_op jit(solution)/shard_map/ppermute | solution.py:19
  143.7 7.0 %copy-start.2 = (bf16[512,384]{1,0:T(8,128)(2,1)S(1)}, bf16[512,384]{1,0:T(8,128)(2,1)}, u32[]{:S(2)}) copy-start(bf16[512,384]{1,0:T(8,128)(2,1)} %add_convert_fusion.1) | copy-start | bytes 1179652
  143.7 7.0 %collective-permute-start.4 = (bf16[8,1536]{1,0:T(8,128)(2,1)S(1)}, bf16[8,1536]{1,0:T(8,128)(2,1)S(1)}, u32[]{:S(2)}, u32[]{:S(2)}) collective-permute-start(bf16[8,1536]{1,0:T(8,128)(2,1)S(1)} %get-tuple-element.5), channel_id=1, source_target_pairs={{0,4},{4,8},{8,12},{12,16},{16,20},{20,24},{24,28},{28,32},{32,36}... | collective-permute-start | bytes 73736 | tf_op jit(solution)/shard_map/ppermute | solution.py:18
  150.6 2.4 copy-start.4
  150.6 154.0 %copy-start.5 = (bf16[384,384]{1,0:T(8,128)(2,1)S(1)}, bf16[384,384]{1,0:T(8,128)(2,1)}, u32[]{:S(2)}) copy-start(bf16[384,384]{1,0:T(8,128)(2,1)} %param.10) | copy-start | bytes 884740
  154.3 192.1 %all-reduce.5.cloned.1.call-start = ((), (), s32[]{:S(2)}) async-start(), calls=%async_computation.4 | async-start | bytes 1179648 | tf_op jit(solution)/shard_map/psum | solution.py:64
Sparse Core Ops, SparseCore 0:
  10.5 29.3 all-gather.3
  58.9 28.6 all-gather.5
  106.0 29.3 all-gather.7
  154.4 150.2 all-reduce.2
  307.3 39.0 all-reduce.4
